TPU v7x, 256 devices: a whole 4x4x8 slice. The times are simulated.
256 devices in a mesh: row: 32 (over x, y, core), col: 8 (over z).
Axes of the slice: x: 4, y: 4, z: 8, core: 2. Of those that a mesh axis runs over, the one named last changes fastest.
Arguments:
- block_values: bfloat16 [32, 8, 192, 128, 128], P('row', 'col'), may hold values from -0.0625 to 0.0625
- block_rows: int32 [32, 8, 192], P('row', 'col'), may hold values from 0 to 4095, as said below
- block_cols: int32 [32, 8, 192], P('row', 'col'), may hold values from 0 to 4095, as said below
- block_counts: int32 [32, 8], P('row', 'col'), may hold values from 48 to 192, as said below
- precond: float32 [8, 512, 128, 128], P('col', 'row')
- right_side: float32 [8, 512, 32, 128], P('col', 'row'), may hold values from -6 to 6
Outputs:
- solution: float32 [8, 512, 32, 128], P('col', 'row')
Inputs may be any that keep to these rules, and one draw needn't show every extreme that they name: `block_rows`: the block rows of device (r, c) lie in [c * 512, (c + 1) * 512); positions may repeat; for each j, at most 9 of a device's 192 slots have (row mod 512) // 16 == j, and in every index of col some j has exactly 9 such slots on every device. `block_cols`: every block column q of device (r, c) has (q mod 512) // 16 == r; positions may repeat. `block_counts`: slots at or past a device's count are unused; some device uses all 192 slots.
All inputs are finite; a program needn't handle non-finite values.
Results may differ from a plain program's by a relative error of at most 0.00073.
Values may be sent and summed in bfloat16 or wider, within the bound.
A program may use at most 64 MiB of HBM per device.

v0:
```python
import jax
import jax.numpy as jnp
from jax import lax
from jax.sharding import PartitionSpec as P

ITERS = 3


def apply_blocks(matrix, field):
    return jnp.einsum("poi,pki->pko", matrix, field, precision=lax.Precision.HIGHEST)


def block_terms(vectors, values, col_local):
    gathered = vectors[col_local]
    return jnp.einsum("ski,soi->sko", gathered, values, preferred_element_type=jnp.float32)


def per_device(block_values, block_rows, block_cols, block_counts, precond, right_side):
    owned = right_side.shape[1]
    row_devices = lax.axis_size("row")
    group = owned * row_devices
    slot_total = block_values.shape[2]
    values = block_values[0, 0]
    row_local = block_rows[0, 0] % group
    col_global = block_cols[0, 0]
    col_local = col_global // group * owned + col_global % owned
    used = block_counts[0, 0]
    live = jnp.arange(slot_total, dtype=jnp.int32) < used
    inverse = precond[0]
    rhs_own = right_side[0]
    solution = apply_blocks(inverse, rhs_own)
    for step in range(ITERS):
        pieces = lax.all_gather(solution.astype(jnp.bfloat16)[None], "col", axis=1, tiled=True)[0]
        terms = block_terms(pieces, values, col_local)
        terms = jnp.where(live[:, None, None], terms, jnp.zeros_like(terms))
        partial_value = jax.ops.segment_sum(terms, row_local, num_segments=group)
        product = lax.psum_scatter(partial_value, "row", scatter_dimension=0, tiled=True)
        residual = rhs_own - solution - product
        solution = solution + apply_blocks(inverse, residual)
    return solution[None]


def solution(mesh):
    placed = (
        P("row", "col", None, None, None),
        P("row", "col", None),
        P("row", "col", None),
        P("row", "col"),
        P("col", "row", None, None),
        P("col", "row", None, None),
    )
    return jax.shard_map(
        per_device,
        mesh=mesh,
        in_specs=placed,
        out_specs=P("col", "row", None, None),
        check_vma=False,
    )
```

profile of v0, /device:TPU:1, one launch (start us, length us, event | category | flops | bytes accessed | tf_op | source)
XLA Modules:
  0.0 562.0 jit_solution(1981962366836233417)
XLA Ops:
  6.5 1.2 copy-done
  7.8 3.3 fusion.30
  11.8 0.7 compare_select_fusion
  13.2 35.2 %all-gather.7.cloned.1.call-done = bf16[128,32,128]{2,1,0:T(8,128)(2,1)} async-done(((bf16[16,32,128]{2,1,0:T(8,128)(2,1)}), bf16[128,32,128]{2,1,0:T(8,128)(2,1)}) %all-gather.7.cloned.1.call-update) | async-done | bytes 1048592 | tf_op jit(solution)/shard_map/all_gather | solution.py:33
  48.5 2.1 gather_fusion
  50.6 7.9 %fusion.6 = f32[192,32,128]{2,1,0:T(8,128)} fusion(bf16[192,32,128]{2,1,0:T(8,128)(2,1)S(1)} %gather_fusion, bf16[1,1,192,128,128]{4,3,2,1,0:T(8,128)(2,1)} %param.6, pred[192]{0:T(512)(128)(4,1)S(1)} %iota_compare_fusion), kind=kOutput, calls=%fused_computation.12 | convolution fusion | flops 202113024 | bytes 11010240 | tf_op jit(solution)/shard_map/ski,soi->sko/dot_general | solution.py:15
  58.5 4.3 broadcast.156.clone
  62.8 25.9 %scatter_fusion = f32[512,32,128]{2,1,0:T(8,128)} fusion(f32[512,32,128]{2,1,0:T(8,128)} %broadcast.156.clone, s32[192]{0:T(256)S(1)} %bitcast.73, f32[192,32,128]{2,1,0:T(8,128)} %fusion.6), kind=kCustom, calls=%fused_computation.3 | custom fusion | flops 786432 | bytes 9437952 | tf_op jit(solution)/shard_map/scatter-add | solution.py:36
  88.7 102.2 %reduce-scatter.4.cloned.1.call-done = f32[16,32,128]{2,1,0:T(8,128)} async-done(((f32[512,32,128]{2,1,0:T(8,128)}), f32[16,32,128]{2,1,0:T(8,128)}) %reduce-scatter.4.cloned.1.call-update) | async-done | bytes 262160 | tf_op jit(solution)/shard_map/reduce_scatter | solution.py:37
  190.9 3.3 fusion.31
  194.3 34.6 %all-gather.9.cloned.1.call-done = bf16[128,32,128]{2,1,0:T(8,128)(2,1)} async-done(((bf16[16,32,128]{2,1,0:T(8,128)(2,1)}), bf16[128,32,128]{2,1,0:T(8,128)(2,1)}) %all-gather.9.cloned.1.call-update) | async-done | bytes 1048592 | tf_op jit(solution)/shard_map/all_gather | solution.py:33
  228.9 2.1 gather_fusion.1
  231.0 7.9 %fusion.9 = f32[192,32,128]{2,1,0:T(8,128)} fusion(bf16[192,32,128]{2,1,0:T(8,128)(2,1)S(1)} %gather_fusion.1, bf16[1,1,192,128,128]{4,3,2,1,0:T(8,128)(2,1)} %param.6, pred[192]{0:T(512)(128)(4,1)S(1)} %iota_compare_fusion), kind=kOutput, calls=%fused_computation.13 | convolution fusion | flops 202113024 | bytes 11010240 | tf_op jit(solution)/shard_map/ski,soi->sko/dot_general | solution.py:15
  238.9 4.3 broadcast.156.clone.1
  243.2 25.9 %scatter_fusion.1 = f32[512,32,128]{2,1,0:T(8,128)} fusion(f32[512,32,128]{2,1,0:T(8,128)} %broadcast.156.clone.1, s32[192]{0:T(256)S(1)} %bitcast.74, f32[192,32,128]{2,1,0:T(8,128)} %fusion.9), kind=kCustom, calls=%fused_computation.4 | custom fusion | flops 786432 | bytes 9437952 | tf_op jit(solution)/shard_map/scatter-add | solution.py:36
  269.2 102.2 %reduce-scatter.6.cloned.1.call-done = f32[16,32,128]{2,1,0:T(8,128)} async-done(((f32[512,32,128]{2,1,0:T(8,128)}), f32[16,32,128]{2,1,0:T(8,128)}) %reduce-scatter.6.cloned.1.call-update) | async-done | bytes 262160 | tf_op jit(solution)/shard_map/reduce_scatter | solution.py:37
  371.3 3.3 fusion.32
  374.9 34.4 %all-gather.11.cloned.1.call-done = bf16[128,32,128]{2,1,0:T(8,128)(2,1)} async-done(((bf16[16,32,128]{2,1,0:T(8,128)(2,1)}), bf16[128,32,128]{2,1,0:T(8,128)(2,1)}) %all-gather.11.cloned.1.call-update) | async-done | bytes 1048592 | tf_op jit(solution)/shard_map/all_gather | solution.py:33
  409.3 2.1 gather_fusion.2
  411.4 7.9 %fusion.12 = f32[192,32,128]{2,1,0:T(8,128)} fusion(bf16[192,32,128]{2,1,0:T(8,128)(2,1)S(1)} %gather_fusion.2, bf16[1,1,192,128,128]{4,3,2,1,0:T(8,128)(2,1)} %param.6, pred[192]{0:T(512)(128)(4,1)S(1)} %iota_compare_fusion), kind=kOutput, calls=%fused_computation.14 | convolution fusion | flops 202113024 | bytes 11010240 | tf_op jit(solution)/shard_map/ski,soi->sko/dot_general | solution.py:15
  419.3 4.3 broadcast.156
  423.6 25.9 %scatter_fusion.2 = f32[512,32,128]{2,1,0:T(8,128)} fusion(f32[512,32,128]{2,1,0:T(8,128)} %broadcast.156, s32[192]{0:T(256)S(1)} %bitcast.75, f32[192,32,128]{2,1,0:T(8,128)} %fusion.12), kind=kCustom, calls=%fused_computation.5 | custom fusion | flops 786432 | bytes 9437952 | tf_op jit(solution)/shard_map/scatter-add | solution.py:36
  449.5 102.2 %reduce-scatter.8.cloned.1.call-done = f32[16,32,128]{2,1,0:T(8,128)} async-done(((f32[512,32,128]{2,1,0:T(8,128)}), f32[16,32,128]{2,1,0:T(8,128)}) %reduce-scatter.8.cloned.1.call-update) | async-done | bytes 262160 | tf_op jit(solution)/shard_map/reduce_scatter | solution.py:37
  551.7 3.4 fusion.15
  (18 shorter events, 1.2 us)
Async XLA Ops:
  6.5 1.2 copy-start
  6.5 41.9 %all-gather.7.cloned.1.call-start = ((), (), s32[]{:S(2)}) async-start(), calls=%async_computation.6 | async-start | bytes 1179648 | tf_op jit(solution)/shard_map/all_gather | solution.py:33
  11.1 179.8 %reduce-scatter.4.cloned.1.call-start = ((), (), s32[]{:S(2)}) async-start(), calls=%async_computation.3 | async-start | bytes 8650752 | tf_op jit(solution)/shard_map/reduce_scatter | solution.py:37
  88.7 102.2 %copy-start.1 = (f32[1,16,32,128]{3,2,1,0:T(8,128)S(1)}, f32[1,16,32,128]{3,2,1,0:T(8,128)}, u32[]{:S(2)}) copy-start(f32[1,16,32,128]{3,2,1,0:T(8,128)} %param.11) | copy-start | bytes 786436
  88.7 140.2 %all-gather.9.cloned.1.call-start = ((), (), s32[]{:S(2)}) async-start(), calls=%async_computation.7 | async-start | bytes 1179648 | tf_op jit(solution)/shard_map/all_gather | solution.py:33
  194.3 177.1 %reduce-scatter.6.cloned.1.call-start = ((), (), s32[]{:S(2)}) async-start(), calls=%async_computation.4 | async-start | bytes 8650752 | tf_op jit(solution)/shard_map/reduce_scatter | solution.py:37
  269.1 140.2 %all-gather.11.cloned.1.call-start = ((), (), s32[]{:S(2)}) async-start(), calls=%async_computation.8 | async-start | bytes 1179648 | tf_op jit(solution)/shard_map/all_gather | solution.py:33
  374.7 177.1 %reduce-scatter.8.cloned.1.call-start = ((), (), s32[]{:S(2)}) async-start(), calls=%async_computation.5 | async-start | bytes 8650752 | tf_op jit(solution)/shard_map/reduce_scatter | solution.py:37
Sparse Core Ops, SparseCore 0:
  11.2 37.1 all-gather.6
  88.8 102.0 reduce-scatter.3
  194.4 34.4 all-gather.8
  269.2 102.0 reduce-scatter.5
  374.8 34.4 all-gather.10
  449.7 102.0 reduce-scatter.7
where the time goes:
time: 564 us; the launch traced here: 562 us
  waiting for transfers between devices  411 us (73%)
  other arithmetic  79 us (14%)
  matrix products  37.1 us (7%)
  local copies, waits for them, and re-layouts  20.5 us (4%)
  between operations  14.2 us (3%)
    reduce_scatter x3, waiting for transfers between devices, per_device(): lax.psum_scatter(partial_value, 'row', scatter_dimension=0, tiled=True)  307 us
    all_gather x3, waiting for transfers between devices, per_device(): lax.all_gather(solution.astype(jnp.bfloat16)[None], 'col', axis=1, tiled=...  104 us
    scatter-add x3, other arithmetic, per_device(): partial_value = jax.ops.segment_sum(terms, row_local, num_segments=group)  77.6 us
    dot_general x3, matrix products, block_terms(): jnp.einsum('ski,soi->sko', gathered, values, preferred_element_type=jnp.f...  23.7 us
    dot_general x4, matrix products, apply_blocks(): jnp.einsum('poi,pki->pko', matrix, field, precision=lax.Precision.HIGHEST)  13.4 us
    another operation x3, local copies, waits for them, and re-layouts  12.9 us
  transfers between devices with their start and end apart: 6, of which 6 were waited for; matrix products, arithmetic and copies ran while one was open for 0% of the time, Pallas kernels for 0%

commit v1 on v0

v1 whole, which is shorter than its diff:
```python
import functools

import jax
import jax.numpy as jnp
from jax import lax
from jax.experimental import pallas as pl
from jax.experimental.pallas import tpu as pltpu
from jax.sharding import PartitionSpec as P

ITERS = 3
GROUPS = 2
CHUNK = 48
WIDE = 2
MESH = pl.DeviceIdType.MESH
F32 = jnp.float32
BF16 = jnp.bfloat16


def tables(rows, cols, count, group, owned):
    slots = rows.shape[0]
    me = lax.axis_index("row")
    my_x, my_y, my_core = me // 8, (me // 2) % 4, me % 2
    local = rows % group
    dest, inner = local // owned, local % owned
    to_x, to_y, to_core = dest // 8, (dest // 2) % 4, dest % 2
    part, block = inner // 8, inner % 8
    gray = lambda v: v ^ (v >> 1)
    off_x, off_y = gray(to_x) ^ gray(my_x), gray(to_y) ^ gray(my_y)
    bits = off_x % 2 + 2 * (off_y % 2) + 4 * (off_x // 2) + 8 * (off_y // 2)
    place = jnp.zeros_like(dest)
    for stage in range(4):
        dim = (to_core + stage + 2 * part) % 4
        place = 2 * place + ((bits >> dim) & 1)
    own = (to_core == my_core).astype(jnp.int32)
    key = ((own * 2 + part) * 16 + place) * 8 + block
    ids = jnp.arange(slots, dtype=jnp.int32)
    key = jnp.where(ids < count, key, 512)
    full = key * 256 + ids
    rank = jnp.sum((full[None, :] < full[:, None]).astype(jnp.int32), axis=1)
    hot = rank[None, :] == ids[:, None]
    col_local = cols // group * owned + cols % owned
    pick = lambda v: jnp.sum(jnp.where(hot, v[None, :], 0), axis=1)
    slot_sorted, col_sorted, key_sorted = pick(ids), pick(col_local), pick(key)
    before = jnp.concatenate([jnp.full((1,), -1, jnp.int32), key_sorted[:-1]])
    keep = (key_sorted == before).astype(F32)
    places = jnp.arange(512, dtype=jnp.int32)
    upto = jnp.sum((key[None, :] <= places[:, None]).astype(jnp.int32), axis=1)
    here = jnp.sum((key[None, :] == places[:, None]).astype(jnp.int32), axis=1)
    last = jnp.where(here > 0, upto - 1, slots)
    return slot_sorted, col_sorted, keep, last


def kernel(slot, col, keep, last, values, precond, rhs, out,
           blocks, weights, xall, xuse, sums, osend, orecv, hsend, hrecv, wsend, wrecv,
           load_sem, ag_send, ag_recv, o_send, o_recv, h_send, h_recv):
    slots = values.shape[0]
    owned, wide = rhs.shape[0], rhs.shape[1]
    k = wide // GROUPS
    row, z = lax.axis_index("row"), lax.axis_index("col")
    x, y, core = row // 8, (row // 2) % 4, row % 2
    zr, zl = (z + 1) % 8, (z + 7) % 8

    def torus(dim):
        is_x, is_a = 1 - dim % 2, 1 - dim // 2
        nx = x + is_x * (is_a * (1 - 2 * (x % 2)) + (1 - is_a) * (3 - 2 * x))
        ny = y + (1 - is_x) * (is_a * (1 - 2 * (y % 2)) + (1 - is_a) * (3 - 2 * y))
        return ((nx * 4 + ny) * 2 + core, z)

    right, left = (row, zr), (row, zl)
    twin = ((x * 4 + y) * 2 + 1 - core, z)

    load = pltpu.make_async_copy(values, blocks, load_sem)
    load.start()

    barrier = pltpu.get_barrier_semaphore()
    for peer in (right, left, twin, torus(0), torus(1), torus(2), torus(3)):
        pl.semaphore_signal(barrier, inc=1, device_id=peer, device_id_type=MESH)

    def ring(n, g, way, hop):
        if way == 0:
            owner, peer = (z + 8 - (hop - 1)) % 8, right
        else:
            owner, peer = (z + (hop - 1)) % 8, left
        ref = xall.at[n, g, owner]
        if hop == 4:
            ref = ref.at[pl.ds(8 * way, 8)]
        return pltpu.make_async_remote_copy(
            src_ref=ref, dst_ref=ref,
            send_sem=ag_send.at[n, g, way, hop - 1], recv_sem=ag_recv.at[n, g, way, hop - 1],
            device_id=peer, device_id_type=MESH)

    def ring_in(n, g, way, hop):
        owner = (z + 8 - hop) % 8 if way == 0 else (z + hop) % 8
        ref = xall.at[n, g, owner]
        if hop == 4:
            ref = ref.at[pl.ds(8 * way, 8)]
        peer = right if way == 0 else left
        return pltpu.make_async_remote_copy(
            src_ref=ref, dst_ref=ref,
            send_sem=ag_send.at[n, g, way, hop - 1], recv_sem=ag_recv.at[n, g, way, hop - 1],
            device_id=peer, device_id_type=MESH)

    def twin_copy(n, g):
        return pltpu.make_async_remote_copy(
            src_ref=osend.at[g], dst_ref=orecv.at[n % 2, g],
            send_sem=o_send.at[n, g], recv_sem=o_recv.at[n, g],
            device_id=twin, device_id_type=MESH)

    def half_copy(n, g, m, t):
        h = 8 >> t
        source, target = (wsend, wrecv) if t >= WIDE else (hsend, hrecv)
        return pltpu.make_async_remote_copy(
            src_ref=source.at[g, m, pl.ds(h, h)], dst_ref=target.at[n, g, m, pl.ds(h, h)],
            send_sem=h_send.at[n, g, m, t], recv_sem=h_recv.at[n, g, m, t],
            device_id=torus((core + t + 2 * m) % 4), device_id_type=MESH)

    def apply(r, b):
        hi = r.astype(BF16)
        lo = (r - hi.astype(F32)).astype(BF16)
        both = lax.dot_general(jnp.concatenate([hi, lo], 0), weights[b],
                               (((1,), (0,)), ((), ())), preferred_element_type=F32)
        return both[:k, :128] + (both[:k, 128:] + both[k:, :128])

    def start_ring(n, g):
        ring(n, g, 0, 1).start()
        ring(n, g, 1, 1).start()

    for b in range(owned):
        turned = precond[b].T
        hi = turned.astype(BF16)
        lo = (turned - hi.astype(F32)).astype(BF16)
        weights[b] = jnp.concatenate([hi, lo], 1)
    for g in range(GROUPS):
        span = pl.ds(g * k, k)
        for b in range(owned):
            first = apply(rhs[b, span, :], b)
            out[b, span, :] = first
            xall[0, g, z, b] = first.astype(BF16)
        sums[g, slots] = jnp.zeros((k, 128), F32)
    pl.semaphore_wait(barrier, 7)
    for g in range(GROUPS):
        start_ring(0, g)
    load.wait()

    def products(g, first, count):
        def dots(c, carry):
            for u in range(0, CHUNK, 2):
                s = c * CHUNK + u
                pair = jnp.concatenate([blocks[slot[s]], blocks[slot[s + 1]]], 0)
                field = jnp.concatenate([xuse[g, col[s]], xuse[g, col[s + 1]]], 0)
                r = lax.dot_general(field, pair, (((1,), (1,)), ((), ())), preferred_element_type=F32)
                sums[g, s] = r[:k, :128]
                sums[g, s + 1] = r[k:, 128:]
            return carry

        lax.fori_loop(first, first + count, dots, 0)

    def running(g, first, count, carry):
        def step(c, total):
            for u in range(16):
                s = c * 16 + u
                total = sums[g, s] + keep[s] * total
                sums[g, s] = total
            return total

        return lax.fori_loop(first, first + count, step, carry)

    def total_of(n, g, m, d, b, stages):
        v = sums[g, last[256 + (m * 16 + d) * 8 + b]] + orecv[n % 2, g, m * 16 + d, b]
        for t in range(stages):
            source = wrecv if t >= WIDE else hrecv
            v = v + source[n, g, m, (8 >> t) + d, b].astype(F32)
        return v

    def iteration(n, carry):
        for hop in range(1, 4):
            for g in range(GROUPS):
                for way in range(2):
                    ring_in(n, g, way, hop).wait_recv()
                    ring(n, g, way, hop + 1).start()
        for g in range(GROUPS):
            for way in range(2):
                ring_in(n, g, way, 4).wait_recv()

            def take(c, a):
                for b in range(owned):
                    xuse[g, c * owned + b] = xall[n, g, c, b]
                return a

            lax.fori_loop(0, 8, take, 0)
            products(g, 0, 3)
            run = running(g, 0, 9, jnp.zeros((k, 128), F32))

            def other(c, a):
                for b in range(8):
                    osend[g, c, b] = sums[g, last[c * 8 + b]]
                return a

            lax.fori_loop(0, 32, other, 0)
            twin_copy(n, g).start()
            products(g, 3, 1)
            running(g, 9, 3, run)
        for t in range(4):
            for g in range(GROUPS):
                if t == 0:
                    twin_copy(n, g).wait_recv()
                for m in range(2):
                    if t > 0:
                        half_copy(n, g, m, t - 1).wait_recv()

                    def send(d, a):
                        for b in range(8):
                            v = total_of(n, g, m, d, b, t)
                            if t >= WIDE:
                                wsend[g, m, d, b] = v
                            else:
                                hsend[g, m, d, b] = v.astype(BF16)
                        return a

                    lax.fori_loop(8 >> t, 16 >> t, send, 0)
                    half_copy(n, g, m, t).start()
        for g in range(GROUPS):
            span = pl.ds(g * k, k)
            for m in range(2):
                half_copy(n, g, m, 3).wait_recv()
            for b in range(owned):
                now = out[b, span, :]
                residual = rhs[b, span, :] - now - total_of(n, g, b // 8, 0, b % 8, 4)
                now = now + apply(residual, b)
                out[b, span, :] = now

                @pl.when(n < ITERS - 1)
                def _():
                    xall[n + 1, g, z, b] = now.astype(BF16)

            @pl.when(n < ITERS - 1)
            def _():
                start_ring(n + 1, g)

        for g in range(GROUPS):
            for way in range(2):
                for hop in range(1, 5):
                    ring(n, g, way, hop).wait_send()
            twin_copy(n, g).wait_send()
            for m in range(2):
                for t in range(4):
                    half_copy(n, g, m, t).wait_send()
        return carry

    lax.fori_loop(0, ITERS, iteration, 0)


def per_device(block_values, block_rows, block_cols, block_counts, precond, right_side):
    owned, wide, bs = right_side.shape[1:]
    slots = block_values.shape[2]
    group = owned * lax.axis_size("row")
    k = wide // GROUPS
    index = tables(block_rows[0, 0], block_cols[0, 0], block_counts[0, 0], group, owned)
    vmem = pl.BlockSpec(memory_space=pltpu.VMEM)
    smem = pl.BlockSpec(memory_space=pltpu.SMEM)
    dma = pltpu.SemaphoreType.DMA
    result = pl.pallas_call(
        kernel,
        out_shape=jax.ShapeDtypeStruct((owned, wide, bs), F32),
        in_specs=[smem] * 4 + [pl.BlockSpec(memory_space=pl.ANY), vmem, vmem],
        out_specs=vmem,
        scratch_shapes=[
            pltpu.VMEM((slots, bs, bs), BF16),
            pltpu.VMEM((owned, bs, 2 * bs), BF16),
            pltpu.VMEM((ITERS, GROUPS, 8, owned, k, bs), BF16),
            pltpu.VMEM((GROUPS, 8 * owned, k, bs), BF16),
            pltpu.VMEM((GROUPS, slots + 1, k, bs), F32),
            pltpu.VMEM((GROUPS, 32, 8, k, bs), F32),
            pltpu.VMEM((2, GROUPS, 32, 8, k, bs), F32),
            pltpu.VMEM((GROUPS, 2, 16, 8, k, bs), BF16),
            pltpu.VMEM((ITERS, GROUPS, 2, 16, 8, k, bs), BF16),
            pltpu.VMEM((GROUPS, 2, 16 >> WIDE, 8, k, bs), F32),
            pltpu.VMEM((ITERS, GROUPS, 2, 16 >> WIDE, 8, k, bs), F32),
            dma,
            dma((ITERS, GROUPS, 2, 4)), dma((ITERS, GROUPS, 2, 4)),
            dma((ITERS, GROUPS)), dma((ITERS, GROUPS)),
            dma((ITERS, GROUPS, 2, 4)), dma((ITERS, GROUPS, 2, 4)),
        ],
        compiler_params=pltpu.CompilerParams(
            collective_id=0, has_side_effects=True, vmem_limit_bytes=58 << 20),
    )(*index, block_values[0, 0], precond[0], right_side[0])
    return result[None]


def solution(mesh):
    placed = (
        P("row", "col", None, None, None),
        P("row", "col", None),
        P("row", "col", None),
        P("row", "col"),
        P("col", "row", None, None),
        P("col", "row", None, None),
    )
    return jax.shard_map(
        per_device,
        mesh=mesh,
        in_specs=placed,
        out_specs=P("col", "row", None, None),
        check_vma=False,
    )
```

time: 564 us -> 155 us (0.27)
  waiting for transfers between devices: 411 us -> 0 us
  Pallas kernels: 0 us -> 148 us
  other arithmetic: 79 us -> 3.14 us
  matrix products: 37.1 us -> 0 us
  local copies, waits for them, and re-layouts: 20.5 us -> 1.67 us
  between operations: 14.2 us -> 0.67 us
    reduce_scatter x3 -> x0, waiting for transfers between devices: 307 us -> none  [per_device(): lax.psum_scatter(partial_value, 'row', scatter_dimension=0, tiled=True)]
    pallas_call x0 -> x1, Pallas kernels: none -> 148 us  [per_device(): pl.pallas_call(kernel, out_shape=jax.ShapeDtypeStruct((owned, wide, bs),...]
    all_gather x3 -> x0, waiting for transfers between devices: 104 us -> none  [per_device(): lax.all_gather(solution.astype(jnp.bfloat16)[None], 'col', axis=1, tiled=...]
    scatter-add x3 -> x0, other arithmetic: 77.6 us -> none  [per_device(): partial_value = jax.ops.segment_sum(terms, row_local, num_segments=group)]
    dot_general x7 -> x0, matrix products: 37.1 us -> none  [the longest x3 23.7 us: block_terms(): jnp.einsum('ski,soi->sko', gathered, values, preferred_element_type=jnp.f...]
    another operation x3 -> x0, local copies, waits for them, and re-layouts: 12.9 us -> none
    gather x3 -> x0, local copies, waits for them, and re-layouts: 6.36 us -> none  [block_terms(): gathered = vectors[col_local]]
  transfers between devices with their start and end apart: 6 -> 0, of which waited for: 6 -> 0; matrix products, arithmetic and copies ran while one was open for 0% -> 0% of each run, Pallas kernels for 0% -> 0%
where the time goes in v1:
time: 155 us; the launch traced here: 154 us
  Pallas kernels  148 us (95%)
  other arithmetic  3.14 us (2%)
  local copies, waits for them, and re-layouts  1.67 us (1%)
    pallas_call x1, Pallas kernels, per_device(): pl.pallas_call(kernel, out_shape=jax.ShapeDtypeStruct((owned, wide, bs),...  148 us

profile of v1, /device:TPU:1, one launch (start us, length us, event | category | flops | bytes accessed | tf_op | source)
XLA Modules:
  0.0 153.6 jit_solution(11041714490709224568)
XLA Ops:
  0.7 0.8 iota_add_fusion
  1.4 0.2 convert_reduce_fusion.2
  1.6 0.8 select_reduce_fusion
  2.4 0.7 compare_convert_fusion.keep
  3.1 0.2 convert_reduce_fusion.1
  3.2 0.6 add_select_fusion.last
  3.8 148.2 %shard_map.64 = f32[16,32,128]{2,1,0:T(8,128)} custom-call(s32[192]{0:T(256)} %get-tuple-element.9.slot, s32[192]{0:T(256)} %get-tuple-element.8.col, f32[192]{0:T(256)} %compare_convert_fusion.keep, s32[512]{0:T(512)} %add_select_fusion.last, bf16[192,128,128]{2,1,0:T(8,128)(2,1)} %bitcast.9, f32[16,128,128]{2,1,0:T(8,128)} %bitcast.10, f32[16,32,128]{2,1,0:T(8,128)} %bitcast.12), custom_call_target="tpu_custom_call" | custom-call | tf_op jit(solution)/shard_map/pallas_call | solution.py:262
  152.0 1.7 %copy.9 = f32[1,16,32,128]{3,2,1,0:T(8,128)} copy(f32[1,16,32,128]{3,2,1,0:T(8,128)} %bitcast.11) | data formatting | bytes 524288

commit v2 on v0

v2 whole, which is shorter than its diff:
```python
import functools

import jax
import jax.numpy as jnp
from jax import lax
from jax.experimental import pallas as pl
from jax.experimental.pallas import tpu as pltpu
from jax.sharding import PartitionSpec as P

ITERS = 3
GROUPS = 2
CHUNK = 48
RINGP = 2
RINGB = 8
WIDE = 2
MESH = pl.DeviceIdType.MESH
F32 = jnp.float32
BF16 = jnp.bfloat16


def tables(rows, cols, count, group, owned):
    slots = rows.shape[0]
    me = lax.axis_index("row")
    my_x, my_y, my_core = me // 8, (me // 2) % 4, me % 2
    local = rows % group
    dest, inner = local // owned, local % owned
    to_x, to_y, to_core = dest // 8, (dest // 2) % 4, dest % 2
    part, block = inner // 8, inner % 8
    gray = lambda v: v ^ (v >> 1)
    off_x, off_y = gray(to_x) ^ gray(my_x), gray(to_y) ^ gray(my_y)
    bits = off_x % 2 + 2 * (off_y % 2) + 4 * (off_x // 2) + 8 * (off_y // 2)
    place = jnp.zeros_like(dest)
    for stage in range(4):
        dim = (to_core + stage + 2 * part) % 4
        place = 2 * place + ((bits >> dim) & 1)
    own = (to_core == my_core).astype(jnp.int32)
    key = ((own * 2 + part) * 16 + place) * 8 + block
    ids = jnp.arange(slots, dtype=jnp.int32)
    key = jnp.where(ids < count, key, 512)
    full = key * 256 + ids
    rank = jnp.sum((full[None, :] < full[:, None]).astype(jnp.int32), axis=1)
    hot = rank[None, :] == ids[:, None]
    col_local = cols // group * owned + cols % owned
    pick = lambda v: jnp.sum(jnp.where(hot, v[None, :], 0), axis=1)
    slot_sorted, col_sorted, key_sorted = pick(ids), pick(col_local), pick(key)
    before = jnp.concatenate([jnp.full((1,), -1, jnp.int32), key_sorted[:-1]])
    keep = (key_sorted == before).astype(F32)
    places = jnp.arange(512, dtype=jnp.int32)
    upto = jnp.sum((key[None, :] <= places[:, None]).astype(jnp.int32), axis=1)
    here = jnp.sum((key[None, :] == places[:, None]).astype(jnp.int32), axis=1)
    last = jnp.where(here > 0, upto - 1, slots)
    return slot_sorted, col_sorted, keep, last


def kernel(slot, col, keep, last, values, precond, rhs, out,
           blocks, turned, weights, sums, raw, wsend, wrecv, *rest):
    slots = values.shape[0]
    owned, k = rhs.shape[0], rhs.shape[1] // GROUPS
    rest = list(rest)
    take = lambda count: [rest.pop(0) for _ in range(count)]
    table = lambda: [take(GROUPS) for _ in range(ITERS)]
    xall, osend, orecv, hrecv = table(), table(), table(), table()
    hsend = take(GROUPS)
    load_sem, ag_send, ag_recv, o_send, o_recv, h_send, h_recv = rest
    row, z = lax.axis_index("row"), lax.axis_index("col")
    x, y, core = row // 8, (row // 2) % 4, row % 2

    def torus(dim):
        is_x, is_a = 1 - dim % 2, 1 - dim // 2
        nx = x + is_x * (is_a * (1 - 2 * (x % 2)) + (1 - is_a) * (3 - 2 * x))
        ny = y + (1 - is_x) * (is_a * (1 - 2 * (y % 2)) + (1 - is_a) * (3 - 2 * y))
        return nx, ny

    def beside(dim):
        px, py = torus(dim)
        return ((px * 4 + py) * 2 + core, z)

    def along(way, step):
        return (row, (z + step) % 8 if way == 0 else (z + 8 - step) % 8)

    def across(dim, other):
        (px, py), (qx, qy) = torus(dim), torus(other)
        flip = dim % 2
        return ((((1 - flip) * px + flip * qx) * 4 + (flip * py + (1 - flip) * qy)) * 2 + core, z)

    twin = ((x * 4 + y) * 2 + 1 - core, z)

    load = pltpu.make_async_copy(values, blocks, load_sem)
    load.start()

    barrier = pltpu.get_barrier_semaphore()
    for peer in (along(0, 1), along(1, 1), along(0, 2), along(1, 2), twin, beside(0), beside(1), beside(2), beside(3),
                 across((core + 2) % 4, (core + 3) % 4), across(core, (core + 1) % 4)):
        pl.semaphore_signal(barrier, inc=1, device_id=peer, device_id_type=MESH)

    def ring(n, g, way, far, part, incoming=False):
        back = far if incoming else (0 if far < 3 else 2)
        owner = (z + 8 - back) % 8 if way == 0 else (z + back) % 8
        ref = xall[n][g].at[owner, pl.ds(RINGB * part, RINGB)]
        return pltpu.make_async_remote_copy(
            src_ref=ref, dst_ref=ref,
            send_sem=ag_send.at[n, g, way, far - 1, part], recv_sem=ag_recv.at[n, g, way, far - 1, part],
            device_id=along(way, 2 - far % 2), device_id_type=MESH)

    def twin_copy(n, g, m, part):
        span = pl.ds(m * 16 + 8 * (1 - part), 8)
        return pltpu.make_async_remote_copy(
            src_ref=osend[n][g].at[span], dst_ref=orecv[n][g].at[span],
            send_sem=o_send.at[n, g, m, part], recv_sem=o_recv.at[n, g, m, part],
            device_id=twin, device_id_type=MESH)

    def is_wide(n, t):
        return n == ITERS - 1 and t >= WIDE

    def half_copy(n, g, m, t, d):
        source, target = (wsend.at[g], wrecv.at[g]) if is_wide(n, t) else (hsend[g], hrecv[n][g])
        dim = (core + t + 2 * m) % 4
        after = (dim + 1) % 4
        if t < 2:
            peer = beside(dim)
        else:
            peer = (None, beside(after), beside(dim), across(dim, after))[d]
        return pltpu.make_async_remote_copy(
            src_ref=source.at[m, d], dst_ref=target.at[m, d],
            send_sem=h_send.at[n, g, m, d], recv_sem=h_recv.at[n, g, m, d],
            device_id=peer, device_id_type=MESH)

    def apply(r, b):
        hi = r.astype(BF16)
        lo = (r - hi.astype(F32)).astype(BF16)
        both = lax.dot_general(jnp.concatenate([hi, lo], 0), weights[b],
                               (((1,), (0,)), ((), ())), preferred_element_type=F32)
        return both[:k, :128] + (both[:k, 128:] + both[k:, :128])

    def start_ring(n, g, part):
        for way in range(2):
            ring(n, g, way, 2, part).start()
        if part == RINGP - 1:
            for each in range(RINGP):
                for way in range(2):
                    ring(n, g, way, 1, each).start()

    def put(n, g, b, value):
        out[b, pl.ds(g * k, k), :] = value
        if n < ITERS:
            xall[n][g][z, b] = value.astype(BF16)
            if b % RINGB == RINGB - 1:
                start_ring(n, g, b // RINGB)

    for b in range(owned):
        flat = precond[b].T
        hi = flat.astype(BF16)
        lo = (flat - hi.astype(F32)).astype(BF16)
        weights[b] = jnp.concatenate([hi, lo], 1)
    pl.semaphore_wait(barrier, 11)
    for g in range(GROUPS):
        for b in range(owned):
            put(0, g, b, apply(rhs[b, pl.ds(g * k, k), :], b))
        sums[g, slots] = jnp.zeros((k, 128), F32)
    load.wait()

    def turn(first, count):
        def step(c, a):
            for u in range(8):
                turned[c * 8 + u] = blocks[c * 8 + u].T
            return a

        lax.fori_loop(first, first + count, step, 0)

    def products(n, g, first, count, carry):
        def dots(c, total):
            for u in range(0, CHUNK, 2):
                s = c * CHUNK + u
                pair = jnp.concatenate([turned[slot[s]], turned[slot[s + 1]]], 1)
                ca, cb = col[s], col[s + 1]
                field = jnp.concatenate([xall[n][g][ca // 16, ca % 16], xall[n][g][cb // 16, cb % 16]], 0)
                r = lax.dot_general(field, pair, (((1,), (0,)), ((), ())), preferred_element_type=F32)
                raw[u] = r[:k, :128]
                raw[u + 1] = r[k:, 128:]
            for u in range(CHUNK):
                s = c * CHUNK + u
                total = raw[u] + keep[s] * total
                sums[g, s] = total
            return total

        return lax.fori_loop(first, first + count, dots, carry)

    def total_of(n, g, m, d, b, stages, final=False):
        v = sums[g, last[256 + (m * 16 + d) * 8 + b]] + orecv[n][g][m * 16 + d, b].astype(F32)
        for t in range(stages):
            v = v + hrecv[n][g][m, (8 >> t) + d, b].astype(F32)
        for e in range(1, 4 if final else 1):
            v = v + (wrecv[g, m, e, b] if is_wide(n, 2) else hrecv[n][g][m, e, b].astype(F32))
        return v

    def on_last(way, part):
        return part // (RINGP // 2) == way

    def relay(n, g):
        for part in range(RINGP):
            for way in range(2):
                ring(n, g, way, 2, part, True).wait_recv()
                ring(n, g, way, 3, part).start()
                if on_last(way, part):
                    ring(n, g, way, 4, part).start()

    def gathered(n, g):
        for far in (1, 3, 4):
            for part in range(RINGP):
                for way in range(2):
                    if far < 4 or on_last(way, part):
                        ring(n, g, way, far, part, True).wait_recv()

    def compute(n, g):
        run = products(n, g, 0, 3, jnp.zeros((k, 128), F32))
        for part in range(2):
            for m in range(2):
                def other(c, a):
                    for b in range(8):
                        osend[n][g][c, b] = sums[g, last[c * 8 + b]].astype(osend[n][g].dtype)
                    return a

                first = m * 16 + 8 * (1 - part)
                lax.fori_loop(first, first + 8, other, 0)
                twin_copy(n, g, m, part).start()
        products(n, g, 3, 1, run)

    def exchange(n, g, t):
        top = 16 >> t

        def send(i, a):
            d = top - 1 - i
            for m in range(2):
                if n > 0 and not is_wide(n, t):
                    half_copy(n - 1, g, m, t, d).wait_send()
                for s in range(t):
                    half_copy(n, g, m, s, (8 >> s) + d).wait_recv()
                for b in range(8):
                    v = total_of(n, g, m, d, b, t)
                    if is_wide(n, t):
                        wsend[g, m, d, b] = v
                    else:
                        hsend[g][m, d, b] = v.astype(BF16)
                half_copy(n, g, m, t, d).start()
            return a

        if t < 2:
            for m in range(2):
                twin_copy(n, g, m, t).wait_recv()
            lax.fori_loop(0, 8 >> t, send, 0)
        else:
            for i in range(3):
                send(i, 0)

    def update(n, g):
        for m in range(2):
            for t, d in ((0, 8), (1, 4), (2, 3), (2, 2), (2, 1)):
                half_copy(n, g, m, t, d).wait_recv()
            for b in range(8 * m, 8 * m + 8):
                now = out[b, pl.ds(g * k, k), :]
                residual = rhs[b, pl.ds(g * k, k), :] - now - total_of(n, g, m, 0, b % 8, 2, True)
                put(n + 1, g, b, now + apply(residual, b))

    turn(0, 12)
    for n in range(ITERS):
        if n > 0:
            exchange(n - 1, 1, 0)
        relay(n, 0)
        if n > 0:
            exchange(n - 1, 1, 1)
            exchange(n - 1, 1, 2)
        else:
            turn(12, 12)
        gathered(n, 0)
        compute(n, 0)
        if n > 0:
            update(n - 1, 1)
        exchange(n, 0, 0)
        relay(n, 1)
        exchange(n, 0, 1)
        exchange(n, 0, 2)
        gathered(n, 1)
        compute(n, 1)
        update(n, 0)
    for t in range(3):
        exchange(ITERS - 1, 1, t)
    update(ITERS - 1, 1)

    for n in range(ITERS):
        for g in range(GROUPS):
            for way in range(2):
                for far in range(1, 5):
                    for part in range(RINGP):
                        if far < 4 or on_last(way, part):
                            ring(n, g, way, far, part).wait_send()
            for m in range(2):
                for part in range(2):
                    twin_copy(n, g, m, part).wait_send()
                for t, places in enumerate((range(8, 16), range(4, 8), range(1, 4))):
                    for d in places:
                        if n == ITERS - 1 or is_wide(n + 1, t):
                            half_copy(n, g, m, t, d).wait_send()


def per_device(block_values, block_rows, block_cols, block_counts, precond, right_side):
    owned, wide, bs = right_side.shape[1:]
    slots = block_values.shape[2]
    group = owned * lax.axis_size("row")
    k = wide // GROUPS
    index = tables(block_rows[0, 0], block_cols[0, 0], block_counts[0, 0], group, owned)
    vmem = pl.BlockSpec(memory_space=pltpu.VMEM)
    smem = pl.BlockSpec(memory_space=pltpu.SMEM)
    dma = pltpu.SemaphoreType.DMA
    result = pl.pallas_call(
        kernel,
        out_shape=jax.ShapeDtypeStruct((owned, wide, bs), F32),
        in_specs=[smem] * 4 + [pl.BlockSpec(memory_space=pl.ANY), vmem, vmem],
        out_specs=vmem,
        scratch_shapes=[
            pltpu.VMEM((slots, bs, bs), BF16),
            pltpu.VMEM((slots, bs, bs), BF16),
            pltpu.VMEM((owned, bs, 2 * bs), BF16),
            pltpu.VMEM((GROUPS, slots + 1, k, bs), F32),
            pltpu.VMEM((CHUNK, k, bs), F32)]
        + [pltpu.VMEM((GROUPS, 2, 16 >> WIDE, 8, k, bs), F32)] * 2
        + [pltpu.VMEM((8, owned, k, bs), BF16)] * (ITERS * GROUPS)
        + ([pltpu.VMEM((32, 8, k, bs), BF16)] * ((ITERS - 1) * GROUPS)
           + [pltpu.VMEM((32, 8, k, bs), F32)] * GROUPS) * 2
        + [pltpu.VMEM((2, 16, 8, k, bs), BF16)] * (GROUPS + ITERS * GROUPS)
        + [
            dma,
            dma((ITERS, GROUPS, 2, 4, RINGP)), dma((ITERS, GROUPS, 2, 4, RINGP)),
            dma((ITERS, GROUPS, 2, 2)), dma((ITERS, GROUPS, 2, 2)),
            dma((ITERS, GROUPS, 2, 16)), dma((ITERS, GROUPS, 2, 16)),
        ],
        compiler_params=pltpu.CompilerParams(
            collective_id=0, has_side_effects=True, vmem_limit_bytes=58 << 20),
    )(*index, block_values[0, 0], precond[0], right_side[0])
    return result[None]


def solution(mesh):
    placed = (
        P("row", "col", None, None, None),
        P("row", "col", None),
        P("row", "col", None),
        P("row", "col"),
        P("col", "row", None, None),
        P("col", "row", None, None),
    )
    return jax.shard_map(
        per_device,
        mesh=mesh,
        in_specs=placed,
        out_specs=P("col", "row", None, None),
        check_vma=False,
    )
```

time: 564 us -> 118 us (0.21)
  waiting for transfers between devices: 411 us -> 0 us
  Pallas kernels: 0 us -> 112 us
  other arithmetic: 79 us -> 3.14 us
  matrix products: 37.1 us -> 0 us
  local copies, waits for them, and re-layouts: 20.5 us -> 1.67 us
  between operations: 14.2 us -> 0.67 us
    reduce_scatter x3 -> x0, waiting for transfers between devices: 307 us -> none  [per_device(): lax.psum_scatter(partial_value, 'row', scatter_dimension=0, tiled=True)]
    pallas_call x0 -> x1, Pallas kernels: none -> 112 us  [per_device(): pl.pallas_call(kernel, out_shape=jax.ShapeDtypeStruct((owned, wide, bs),...]
    all_gather x3 -> x0, waiting for transfers between devices: 104 us -> none  [per_device(): lax.all_gather(solution.astype(jnp.bfloat16)[None], 'col', axis=1, tiled=...]
    scatter-add x3 -> x0, other arithmetic: 77.6 us -> none  [per_device(): partial_value = jax.ops.segment_sum(terms, row_local, num_segments=group)]
    dot_general x7 -> x0, matrix products: 37.1 us -> none  [the longest x3 23.7 us: block_terms(): jnp.einsum('ski,soi->sko', gathered, values, preferred_element_type=jnp.f...]
    another operation x3 -> x0, local copies, waits for them, and re-layouts: 12.9 us -> none
    gather x3 -> x0, local copies, waits for them, and re-layouts: 6.36 us -> none  [block_terms(): gathered = vectors[col_local]]
  transfers between devices with their start and end apart: 6 -> 0, of which waited for: 6 -> 0; matrix products, arithmetic and copies ran while one was open for 0% -> 0% of each run, Pallas kernels for 0% -> 0%
where the time goes in v2:
time: 118 us; the launch traced here: 117 us
  Pallas kernels  112 us (95%)
  other arithmetic  3.14 us (3%)
  local copies, waits for them, and re-layouts  1.67 us (1%)
    pallas_call x1, Pallas kernels, per_device(): pl.pallas_call(kernel, out_shape=jax.ShapeDtypeStruct((owned, wide, bs),...  112 us

profile of v2, /device:TPU:1, one launch (start us, length us, event | category | flops | bytes accessed | tf_op | source)
XLA Modules:
  0.0 117.2 jit_solution(17815478107499562231)
XLA Ops:
  0.7 0.8 iota_add_fusion
  1.4 0.2 convert_reduce_fusion.2
  1.6 0.8 select_reduce_fusion
  2.4 0.7 compare_convert_fusion.keep
  3.1 0.2 convert_reduce_fusion.1
  3.2 0.6 add_select_fusion.last
  3.8 111.8 %shard_map.64 = f32[16,32,128]{2,1,0:T(8,128)} custom-call(s32[192]{0:T(256)} %get-tuple-element.9.slot, s32[192]{0:T(256)} %get-tuple-element.8.col, f32[192]{0:T(256)} %compare_convert_fusion.keep, s32[512]{0:T(512)} %add_select_fusion.last, bf16[192,128,128]{2,1,0:T(8,128)(2,1)} %bitcast.9, f32[16,128,128]{2,1,0:T(8,128)} %bitcast.10, f32[16,32,128]{2,1,0:T(8,128)} %bitcast.12), custom_call_target="tpu_custom_call" | custom-call | tf_op jit(solution)/shard_map/pallas_call | solution.py:314
  115.6 1.7 %copy.9 = f32[1,16,32,128]{3,2,1,0:T(8,128)} copy(f32[1,16,32,128]{3,2,1,0:T(8,128)} %bitcast.11) | data formatting | bytes 524288

commit v3 on v2

--- a/solution.py
+++ b/solution.py
@@ -1,5 +1,3 @@
-import functools
-
 import jax
 import jax.numpy as jnp
 from jax import lax
@@ -18,42 +16,49 @@
 BF16 = jnp.bfloat16
 
 
-def tables(rows, cols, count, group, owned):
-    slots = rows.shape[0]
-    me = lax.axis_index("row")
-    my_x, my_y, my_core = me // 8, (me // 2) % 4, me % 2
-    local = rows % group
-    dest, inner = local // owned, local % owned
-    to_x, to_y, to_core = dest // 8, (dest // 2) % 4, dest % 2
-    part, block = inner // 8, inner % 8
+def tables(rows, cols, count, x, y, core, slots):
+    total = lambda v, axis: jnp.sum(v.astype(jnp.int32), axis=axis, keepdims=True)
+    wave = lambda shape, axis: lax.broadcasted_iota(jnp.int32, shape, axis)
     gray = lambda v: v ^ (v >> 1)
-    off_x, off_y = gray(to_x) ^ gray(my_x), gray(to_y) ^ gray(my_y)
-    bits = off_x % 2 + 2 * (off_y % 2) + 4 * (off_x // 2) + 8 * (off_y // 2)
-    place = jnp.zeros_like(dest)
+    local = rows & 511
+    dest, inner = local >> 4, local & 15
+    to_x, to_y, to_core = dest >> 3, (dest >> 1) & 3, dest & 1
+    part, block = inner >> 3, inner & 7
+    off_x = gray(to_x) ^ gray(jnp.full_like(rows, x))
+    off_y = gray(to_y) ^ gray(jnp.full_like(rows, y))
+    flags = (off_x & 1, off_y & 1, off_x >> 1, off_y >> 1)
+    place = jnp.zeros_like(rows)
     for stage in range(4):
-        dim = (to_core + stage + 2 * part) % 4
-        place = 2 * place + ((bits >> dim) & 1)
-    own = (to_core == my_core).astype(jnp.int32)
+        dim = (to_core + stage + 2 * part) & 3
+        bit = jnp.zeros_like(rows)
+        for d in range(4):
+            bit = jnp.where(dim == d, flags[d], bit)
+        place = 2 * place + bit
+    own = jnp.where(to_core == core, 1, 0)
     key = ((own * 2 + part) * 16 + place) * 8 + block
-    ids = jnp.arange(slots, dtype=jnp.int32)
+    ids = wave((1, slots), 1)
     key = jnp.where(ids < count, key, 512)
     full = key * 256 + ids
-    rank = jnp.sum((full[None, :] < full[:, None]).astype(jnp.int32), axis=1)
-    hot = rank[None, :] == ids[:, None]
-    col_local = cols // group * owned + cols % owned
-    pick = lambda v: jnp.sum(jnp.where(hot, v[None, :], 0), axis=1)
-    slot_sorted, col_sorted, key_sorted = pick(ids), pick(col_local), pick(key)
-    before = jnp.concatenate([jnp.full((1,), -1, jnp.int32), key_sorted[:-1]])
-    keep = (key_sorted == before).astype(F32)
-    places = jnp.arange(512, dtype=jnp.int32)
-    upto = jnp.sum((key[None, :] <= places[:, None]).astype(jnp.int32), axis=1)
-    here = jnp.sum((key[None, :] == places[:, None]).astype(jnp.int32), axis=1)
+    near = (cols >> 9) * 16 + (cols & 15)
+    eye = wave((slots, slots), 0) == wave((slots, slots), 1)
+    upright = lambda v: total(jnp.where(eye, v, 0), 1)
+    full_up, near_up = upright(full), upright(near)
+    key_up, ids_up = full_up >> 8, full_up & 255
+    rank = total(jnp.where(full < full_up, 1, 0), 1)
+    lanes = wave((1, 512), 1)
+    pick = lambda hot, v: total(jnp.where(hot, v, 0), 0)
+    hot = rank == lanes
+    slot, col, key_at = pick(hot, ids_up), pick(hot, near_up), pick(hot, key_up)
+    keep = jnp.where(key_at == pick(rank + 1 == lanes, key_up), 1.0, 0.0)
+    upto = total(jnp.where(key_up <= lanes, 1, 0), 0)
+    here = total(jnp.where(key_up == lanes, 1, 0), 0)
     last = jnp.where(here > 0, upto - 1, slots)
-    return slot_sorted, col_sorted, keep, last
-
-
-def kernel(slot, col, keep, last, values, precond, rhs, out,
-           blocks, turned, weights, sums, raw, wsend, wrecv, *rest):
+    line = wave((8, 512), 0)
+    return jnp.where(line == 0, slot, jnp.where(line == 1, col, last)), jnp.broadcast_to(keep, (8, 512))
+
+
+def kernel(rows, cols, count, values, precond, rhs, out,
+           blocks, turned, weights, sums, raw, wsend, wrecv, index_v, keep_v, index, keep, *rest):
     slots = values.shape[0]
     owned, k = rhs.shape[0], rhs.shape[1] // GROUPS
     rest = list(rest)
@@ -61,7 +66,7 @@
     table = lambda: [take(GROUPS) for _ in range(ITERS)]
     xall, osend, orecv, hrecv = table(), table(), table(), table()
     hsend = take(GROUPS)
-    load_sem, ag_send, ag_recv, o_send, o_recv, h_send, h_recv = rest
+    load_sem, index_sem, keep_sem, ag_send, ag_recv, o_send, o_recv, h_send, h_recv = rest
     row, z = lax.axis_index("row"), lax.axis_index("col")
     x, y, core = row // 8, (row // 2) % 4, row % 2
 
@@ -157,6 +162,10 @@
         for b in range(owned):
             put(0, g, b, apply(rhs[b, pl.ds(g * k, k), :], b))
         sums[g, slots] = jnp.zeros((k, 128), F32)
+    index_v[...], keep_v[...] = tables(rows[...], cols[...], count[...], x, y, core, slots)
+    moves = (pltpu.make_async_copy(index_v, index, index_sem), pltpu.make_async_copy(keep_v, keep, keep_sem))
+    for move in moves:
+        move.start()
     load.wait()
 
     def turn(first, count):
@@ -171,22 +180,22 @@
         def dots(c, total):
             for u in range(0, CHUNK, 2):
                 s = c * CHUNK + u
-                pair = jnp.concatenate([turned[slot[s]], turned[slot[s + 1]]], 1)
-                ca, cb = col[s], col[s + 1]
+                pair = jnp.concatenate([turned[index[0, s]], turned[index[0, s + 1]]], 1)
+                ca, cb = index[1, s], index[1, s + 1]
                 field = jnp.concatenate([xall[n][g][ca // 16, ca % 16], xall[n][g][cb // 16, cb % 16]], 0)
                 r = lax.dot_general(field, pair, (((1,), (0,)), ((), ())), preferred_element_type=F32)
                 raw[u] = r[:k, :128]
                 raw[u + 1] = r[k:, 128:]
             for u in range(CHUNK):
                 s = c * CHUNK + u
-                total = raw[u] + keep[s] * total
+                total = raw[u] + keep[0, s] * total
                 sums[g, s] = total
             return total
 
         return lax.fori_loop(first, first + count, dots, carry)
 
     def total_of(n, g, m, d, b, stages, final=False):
-        v = sums[g, last[256 + (m * 16 + d) * 8 + b]] + orecv[n][g][m * 16 + d, b].astype(F32)
+        v = sums[g, index[2, 256 + (m * 16 + d) * 8 + b]] + orecv[n][g][m * 16 + d, b].astype(F32)
         for t in range(stages):
             v = v + hrecv[n][g][m, (8 >> t) + d, b].astype(F32)
         for e in range(1, 4 if final else 1):
@@ -217,7 +226,7 @@
             for m in range(2):
                 def other(c, a):
                     for b in range(8):
-                        osend[n][g][c, b] = sums[g, last[c * 8 + b]].astype(osend[n][g].dtype)
+                        osend[n][g][c, b] = sums[g, index[2, c * 8 + b]].astype(osend[n][g].dtype)
                     return a
 
                 first = m * 16 + 8 * (1 - part)
@@ -262,6 +271,8 @@
                 put(n + 1, g, b, now + apply(residual, b))
 
     turn(0, 12)
+    for move in moves:
+        move.wait()
     for n in range(ITERS):
         if n > 0:
             exchange(n - 1, 1, 0)
@@ -305,16 +316,13 @@
 def per_device(block_values, block_rows, block_cols, block_counts, precond, right_side):
     owned, wide, bs = right_side.shape[1:]
     slots = block_values.shape[2]
-    group = owned * lax.axis_size("row")
     k = wide // GROUPS
-    index = tables(block_rows[0, 0], block_cols[0, 0], block_counts[0, 0], group, owned)
     vmem = pl.BlockSpec(memory_space=pltpu.VMEM)
-    smem = pl.BlockSpec(memory_space=pltpu.SMEM)
     dma = pltpu.SemaphoreType.DMA
     result = pl.pallas_call(
         kernel,
         out_shape=jax.ShapeDtypeStruct((owned, wide, bs), F32),
-        in_specs=[smem] * 4 + [pl.BlockSpec(memory_space=pl.ANY), vmem, vmem],
+        in_specs=[vmem, vmem, vmem, pl.BlockSpec(memory_space=pl.ANY), vmem, vmem],
         out_specs=vmem,
         scratch_shapes=[
             pltpu.VMEM((slots, bs, bs), BF16),
@@ -323,19 +331,21 @@
             pltpu.VMEM((GROUPS, slots + 1, k, bs), F32),
             pltpu.VMEM((CHUNK, k, bs), F32)]
         + [pltpu.VMEM((GROUPS, 2, 16 >> WIDE, 8, k, bs), F32)] * 2
+        + [pltpu.VMEM((8, 512), jnp.int32), pltpu.VMEM((8, 512), F32),
+           pltpu.SMEM((8, 512), jnp.int32), pltpu.SMEM((8, 512), F32)]
         + [pltpu.VMEM((8, owned, k, bs), BF16)] * (ITERS * GROUPS)
         + ([pltpu.VMEM((32, 8, k, bs), BF16)] * ((ITERS - 1) * GROUPS)
            + [pltpu.VMEM((32, 8, k, bs), F32)] * GROUPS) * 2
         + [pltpu.VMEM((2, 16, 8, k, bs), BF16)] * (GROUPS + ITERS * GROUPS)
         + [
-            dma,
+            dma, dma, dma,
             dma((ITERS, GROUPS, 2, 4, RINGP)), dma((ITERS, GROUPS, 2, 4, RINGP)),
             dma((ITERS, GROUPS, 2, 2)), dma((ITERS, GROUPS, 2, 2)),
             dma((ITERS, GROUPS, 2, 16)), dma((ITERS, GROUPS, 2, 16)),
         ],
         compiler_params=pltpu.CompilerParams(
             collective_id=0, has_side_effects=True, vmem_limit_bytes=58 << 20),
-    )(*index, block_values[0, 0], precond[0], right_side[0])
+    )(block_rows[0], block_cols[0], block_counts, block_values[0, 0], precond[0], right_side[0])
     return result[None]
 
 

time: 118 us -> 114 us (0.966)
  other arithmetic: 3.14 us -> 0 us
where the time goes in v3:
time: 114 us
  Pallas kernels  111 us (97%)
  local copies, waits for them, and re-layouts  1.67 us (1%)
    pallas_call x1, Pallas kernels, per_device(): pl.pallas_call(kernel, out_shape=jax.ShapeDtypeStruct((owned, wide, bs),...  111 us

profile of v3, /device:TPU:1, one launch (start us, length us, event | category | flops | bytes accessed | tf_op | source)
XLA Modules:
  0.0 113.6 jit_solution(6901585124726236811)
XLA Ops:
  0.7 111.3 %shard_map.64 = f32[16,32,128]{2,1,0:T(8,128)} custom-call(s32[1,192]{1,0:T(1,128)} %bitcast.10, s32[1,192]{1,0:T(1,128)} %bitcast.11, s32[1,1]{1,0:T(1,128)S(6)} %copy.8.count, bf16[192,128,128]{2,1,0:T(8,128)(2,1)} %bitcast.6, f32[16,128,128]{2,1,0:T(8,128)} %bitcast.7, f32[16,32,128]{2,1,0:T(8,128)} %bitcast.9), custom_call_target="tpu_custom_call" | custom-call | tf_op jit(solution)/shard_map/pallas_call | solution.py:322
  111.9 1.7 %copy.9 = f32[1,16,32,128]{3,2,1,0:T(8,128)} copy(f32[1,16,32,128]{3,2,1,0:T(8,128)} %bitcast.8) | data formatting | bytes 524288

commit v4 on v3

--- a/solution.py
+++ b/solution.py
@@ -7,7 +7,7 @@
 
 ITERS = 3
 GROUPS = 2
-CHUNK = 48
+CHUNK = 72
 RINGP = 2
 RINGB = 8
 WIDE = 2
@@ -158,10 +158,13 @@
         lo = (flat - hi.astype(F32)).astype(BF16)
         weights[b] = jnp.concatenate([hi, lo], 1)
     pl.semaphore_wait(barrier, 11)
-    for g in range(GROUPS):
+
+    def begin(g):
         for b in range(owned):
             put(0, g, b, apply(rhs[b, pl.ds(g * k, k), :], b))
         sums[g, slots] = jnp.zeros((k, 128), F32)
+
+    begin(0)
     index_v[...], keep_v[...] = tables(rows[...], cols[...], count[...], x, y, core, slots)
     moves = (pltpu.make_async_copy(index_v, index, index_sem), pltpu.make_async_copy(keep_v, keep, keep_sem))
     for move in moves:
@@ -176,23 +179,23 @@
 
         lax.fori_loop(first, first + count, step, 0)
 
-    def products(n, g, first, count, carry):
+    def products(n, g, start, count, width, carry):
         def dots(c, total):
-            for u in range(0, CHUNK, 2):
-                s = c * CHUNK + u
+            for u in range(0, width, 2):
+                s = start + c * width + u
                 pair = jnp.concatenate([turned[index[0, s]], turned[index[0, s + 1]]], 1)
                 ca, cb = index[1, s], index[1, s + 1]
                 field = jnp.concatenate([xall[n][g][ca // 16, ca % 16], xall[n][g][cb // 16, cb % 16]], 0)
                 r = lax.dot_general(field, pair, (((1,), (0,)), ((), ())), preferred_element_type=F32)
                 raw[u] = r[:k, :128]
                 raw[u + 1] = r[k:, 128:]
-            for u in range(CHUNK):
-                s = c * CHUNK + u
+            for u in range(width):
+                s = start + c * width + u
                 total = raw[u] + keep[0, s] * total
                 sums[g, s] = total
             return total
 
-        return lax.fori_loop(first, first + count, dots, carry)
+        return lax.fori_loop(0, count, dots, carry)
 
     def total_of(n, g, m, d, b, stages, final=False):
         v = sums[g, index[2, 256 + (m * 16 + d) * 8 + b]] + orecv[n][g][m * 16 + d, b].astype(F32)
@@ -221,7 +224,7 @@
                         ring(n, g, way, far, part, True).wait_recv()
 
     def compute(n, g):
-        run = products(n, g, 0, 3, jnp.zeros((k, 128), F32))
+        run = products(n, g, 0, 2, CHUNK, jnp.zeros((k, 128), F32))
         for part in range(2):
             for m in range(2):
                 def other(c, a):
@@ -232,7 +235,7 @@
                 first = m * 16 + 8 * (1 - part)
                 lax.fori_loop(first, first + 8, other, 0)
                 twin_copy(n, g, m, part).start()
-        products(n, g, 3, 1, run)
+        products(n, g, 2 * CHUNK, 1, slots - 2 * CHUNK, run)
 
     def exchange(n, g, t):
         top = 16 >> t
@@ -281,6 +284,7 @@
             exchange(n - 1, 1, 1)
             exchange(n - 1, 1, 2)
         else:
+            begin(1)
             turn(12, 12)
         gathered(n, 0)
         compute(n, 0)
@@ -292,8 +296,11 @@
         exchange(n, 0, 2)
         gathered(n, 1)
         compute(n, 1)
-        update(n, 0)
-    for t in range(3):
+        if n < ITERS - 1:
+            update(n, 0)
+    exchange(ITERS - 1, 1, 0)
+    update(ITERS - 1, 0)
+    for t in range(1, 3):
         exchange(ITERS - 1, 1, t)
     update(ITERS - 1, 1)
 

time: 114 us -> 111 us (0.974)
  Pallas kernels: 111 us -> 108 us
    pallas_call x1, Pallas kernels: 111 us -> 108 us  [per_device(): pl.pallas_call(kernel, out_shape=jax.ShapeDtypeStruct((owned, wide, bs),...]
where the time goes in v4:
time: 111 us; the launch traced here: 110 us
  Pallas kernels  108 us (97%)
  local copies, waits for them, and re-layouts  1.67 us (2%)
    pallas_call x1, Pallas kernels, per_device(): pl.pallas_call(kernel, out_shape=jax.ShapeDtypeStruct((owned, wide, bs),...  108 us

profile of v4, /device:TPU:1, one launch (start us, length us, event | category | flops | bytes accessed | tf_op | source)
XLA Modules:
  0.0 110.0 jit_solution(14938759763217687342)
XLA Ops:
  0.7 107.7 %shard_map.64 = f32[16,32,128]{2,1,0:T(8,128)} custom-call(s32[1,192]{1,0:T(1,128)} %bitcast.10, s32[1,192]{1,0:T(1,128)} %bitcast.11, s32[1,1]{1,0:T(1,128)S(6)} %copy.8.count, bf16[192,128,128]{2,1,0:T(8,128)(2,1)} %bitcast.6, f32[16,128,128]{2,1,0:T(8,128)} %bitcast.7, f32[16,32,128]{2,1,0:T(8,128)} %bitcast.9), custom_call_target="tpu_custom_call" | custom-call | tf_op jit(solution)/shard_map/pallas_call | solution.py:329
  108.4 1.7 %copy.9 = f32[1,16,32,128]{3,2,1,0:T(8,128)} copy(f32[1,16,32,128]{3,2,1,0:T(8,128)} %bitcast.8) | data formatting | bytes 524288
